TPU v7x, 512 devices: a whole 4x8x8 slice. The times are simulated.
512 devices in a mesh: ctx: 64 (over z_hi, y, core), tp: 8 (over x, z_lo).
Axes of the slice: x: 4, y: 8, z: 8 (z_hi: 4, z_lo: 2; z = z_hi * 2 + z_lo), core: 2. Of those that a mesh axis runs over, the one named last changes fastest.
Arguments:
- query_in: bfloat16 [1024, 16384], P('tp', 'ctx'), may hold values from -6 to 6
- key_in: bfloat16 [1024, 16384], P('tp', 'ctx'), may hold values from -6 to 6
- value_in: bfloat16 [1024, 16384], P('tp', 'ctx'), may hold values from -6 to 6
- short_kernel: float32 [3, 1024, 7], P(None, 'tp'), may hold values from -2 to 2
- basis_weight: float32 [64, 33], replicated, may hold values from -96 to 96
- basis_bias: float32 [64], replicated, may hold values from -3.140625 to 3.140625
- filter_proj: float32 [1024, 64], P('tp'), may hold values from -0.75 to 0.75
- decay_rate: float32 [1024], P('tp'), as said below
- skip_gain: float32 [1024], P('tp'), may hold values from -3 to 3
- grad_out: bfloat16 [1024, 16384], P('tp', 'ctx'), may hold values from -6 to 6
Outputs:
- mixed: bfloat16 [1024, 16384], P('tp', 'ctx')
- grad_query: bfloat16 [1024, 16384], P('tp', 'ctx')
- grad_key: bfloat16 [1024, 16384], P('tp', 'ctx')
- grad_value: bfloat16 [1024, 16384], P('tp', 'ctx')
- grad_proj: float32 [1024, 64], P('tp')
- grad_basis: float32 [64, 33], replicated
Inputs may be any that keep to these rules, and one draw needn't show every extreme that they name: decay_rate is positive in every channel.
All inputs are finite; a program needn't handle non-finite values.
Results may differ from a plain program's by a relative error of at most 0.0066.
Values may be sent and summed in bfloat16 or wider, within the bound.
No kernel may reach another device: no remote copies, remote signals or barrier semaphores. Data moves between devices by JAX's collectives and lax.ppermute only.
A program may use at most 64 MiB of HBM per device.

v0:
```python
import math
import jax
import jax.numpy as jnp
from jax import lax
from jax.sharding import PartitionSpec as P

PRECISE = lax.Precision.HIGHEST


def passed_along(value, axis, steps):
    count = lax.axis_size(axis)
    leading, last = (max(0, -steps), min(count, count - steps))
    return lax.ppermute(value, axis, [(source, source + steps) for source in range(leading, last)])


def features(offset_pos, num_pos, seq_total, num_freq):
    positions = offset_pos + jnp.arange(num_pos, dtype=jnp.int32)
    pieces = [positions.astype(jnp.float32) / seq_total]
    for harmonic in range(1, num_freq + 1):
        angles = (harmonic * positions % seq_total).astype(jnp.float32) * (
            2.0 * math.pi / seq_total
        )
        pieces.append(jnp.cos(angles))
        pieces.append(jnp.sin(angles))
    return jnp.stack(pieces)


def window(decay_rate, offset_pos, num_pos, seq_total):
    positions = (offset_pos + jnp.arange(num_pos, dtype=jnp.int32)).astype(jnp.float32)
    energy = jnp.expm1(-2.0 * decay_rate) / jnp.expm1(-2.0 * decay_rate / seq_total)
    return (
        jnp.exp(-(decay_rate[:, None] * positions[None, :]) / seq_total) / jnp.sqrt(energy)[:, None]
    )


def featurize_rim(signal, before, kernel):
    extended = jnp.concatenate([before, signal], axis=1).astype(jnp.float32)
    num_taps = kernel.shape[1]
    rim_len = num_taps - 1
    num_tok = signal.shape[1]
    result = kernel[:, 0:1] * extended[:, rim_len:]
    for offset in range(1, num_taps):
        result = (
            result
            + kernel[:, offset : offset + 1]
            * extended[:, rim_len - offset : rim_len - offset + num_tok]
        )
    return result


def featurize_back(signal, following, kernel):
    extended = jnp.concatenate([signal, following], axis=1).astype(jnp.float32)
    num_taps = kernel.shape[1]
    num_tok = signal.shape[1]
    result = kernel[:, 0:1] * extended[:, :num_tok]
    for offset in range(1, num_taps):
        result = result + kernel[:, offset : offset + 1] * extended[:, offset : offset + num_tok]
    return result


def tables(num_rows, num_cols, modulus):
    row_ids = jnp.arange(num_rows, dtype=jnp.int32)[:, None]
    col_ids = jnp.arange(num_cols, dtype=jnp.int32)[None, :]
    angles = (row_ids * col_ids % modulus).astype(jnp.float32) * (-2.0 * math.pi / modulus)
    return (jnp.cos(angles), jnp.sin(angles))


def spectrum(signal, outer, twiddle, inner):
    num_chan = signal.shape[0]
    folded = signal.reshape(num_chan, outer[0].shape[1], inner[0].shape[0])
    section_re = jnp.einsum("kt,nts->nks", outer[0], folded, precision=PRECISE)
    section_im = jnp.einsum("kt,nts->nks", outer[1], folded, precision=PRECISE)
    turned_re = section_re * twiddle[0] - section_im * twiddle[1]
    turned_im = section_re * twiddle[1] + section_im * twiddle[0]
    spec_re = jnp.einsum("nks,sj->nkj", turned_re, inner[0], precision=PRECISE) - jnp.einsum(
        "nks,sj->nkj", turned_im, inner[1], precision=PRECISE
    )
    spec_im = jnp.einsum("nks,sj->nkj", turned_re, inner[1], precision=PRECISE) + jnp.einsum(
        "nks,sj->nkj", turned_im, inner[0], precision=PRECISE
    )
    return (spec_re, spec_im)


def restore(spec_re, spec_im, outer, twiddle, inner):
    num_chan = spec_re.shape[0]
    padded_len = outer[0].shape[0] * inner[0].shape[0]
    back_re = jnp.einsum("nkj,sj->nks", spec_re, inner[0], precision=PRECISE) + jnp.einsum(
        "nkj,sj->nks", spec_im, inner[1], precision=PRECISE
    )
    back_im = jnp.einsum("nkj,sj->nks", spec_im, inner[0], precision=PRECISE) - jnp.einsum(
        "nkj,sj->nks", spec_re, inner[1], precision=PRECISE
    )
    turned_re = back_re * twiddle[0] + back_im * twiddle[1]
    turned_im = back_im * twiddle[0] - back_re * twiddle[1]
    result = jnp.einsum("kt,nks->nts", outer[0], turned_re, precision=PRECISE) + jnp.einsum(
        "kt,nks->nts", outer[1], turned_im, precision=PRECISE
    )
    return result.reshape(num_chan, -1) * (1.0 / padded_len)


def convolve_forward(carried_chan, filter_chan, own_skip, transform_tables):
    outer, twiddle, inner = transform_tables
    carried_wide = carried_chan.astype(jnp.float32)
    carried_re, carried_im = spectrum(carried_wide, outer, twiddle, inner)
    filter_re, filter_im = spectrum(filter_chan.astype(jnp.float32), outer, twiddle, inner)
    conv_chan = restore(
        filter_re * carried_re - filter_im * carried_im,
        filter_re * carried_im + filter_im * carried_re,
        outer,
        twiddle,
        inner,
    )
    long_chan = (conv_chan + own_skip[:, None] * carried_wide).astype(jnp.bfloat16)
    return (long_chan, (carried_re, carried_im, filter_re, filter_im))


def convolve_backward(grad_chan, spectra, own_skip, transform_tables):
    outer, twiddle, inner = transform_tables
    carried_re, carried_im, filter_re, filter_im = spectra
    grad_chan_wide = grad_chan.astype(jnp.float32)
    grad_re, grad_im = spectrum(grad_chan_wide, outer, twiddle, inner)
    carried_grad_chan = (
        restore(
            filter_re * grad_re + filter_im * grad_im,
            filter_re * grad_im - filter_im * grad_re,
            outer,
            twiddle,
            inner,
        )
        + own_skip[:, None] * grad_chan_wide
    ).astype(jnp.bfloat16)
    filter_grad_chan = restore(
        carried_re * grad_re + carried_im * grad_im,
        carried_re * grad_im - carried_im * grad_re,
        outer,
        twiddle,
        inner,
    ).astype(jnp.bfloat16)
    return (carried_grad_chan, filter_grad_chan)


def on_device(
    query_in,
    key_in,
    value_in,
    short_kernel,
    basis_weight,
    basis_bias,
    filter_proj,
    decay_rate,
    skip_gain,
    grad_out,
):
    ctx_size = lax.axis_size("ctx")
    ctx_rank = lax.axis_index("ctx")
    tp_size = lax.axis_size("tp")
    num_tok = query_in.shape[1]
    chan_local = query_in.shape[0]
    seq_total = num_tok * ctx_size
    all_channels = chan_local * tp_size
    num_freq = (basis_weight.shape[1] - 1) // 2
    feat_width = basis_weight.shape[0]
    rim_len = short_kernel.shape[2] - 1
    tok_start = ctx_rank * num_tok
    rim_edge = num_tok - rim_len
    per_dev = chan_local // ctx_size
    chan_start = ctx_rank * per_dev
    own_skip = lax.dynamic_slice_in_dim(skip_gain, chan_start, per_dev)
    proj_scale = 1.0 / math.sqrt(seq_total)
    basis_scale = math.sqrt(feat_width / (seq_total * all_channels))
    before = passed_along(
        (query_in[:, rim_edge:], key_in[:, rim_edge:], value_in[:, rim_edge:]), "ctx", 1
    )
    query_feat = featurize_rim(query_in, before[0], short_kernel[0])
    key_feat = featurize_rim(key_in, before[1], short_kernel[1])
    value_feat = featurize_rim(value_in, before[2], short_kernel[2])
    carried = (key_feat * value_feat).astype(jnp.bfloat16)
    grad_wide = grad_out.astype(jnp.float32)
    grad_long = (grad_wide * query_feat).astype(jnp.bfloat16)
    basis_rows = features(tok_start, num_tok, seq_total, num_freq)
    hidden_in = (
        jnp.dot(basis_weight, basis_rows, precision=PRECISE, preferred_element_type=jnp.float32)
        + basis_bias[:, None]
    )
    activation = jnp.sin(hidden_in)
    envelope = window(decay_rate, tok_start, num_tok, seq_total)
    filter_tok = (
        jnp.dot(filter_proj, activation, precision=PRECISE, preferred_element_type=jnp.float32)
        * envelope
    ).astype(jnp.bfloat16)
    inner_len = 2 * ctx_size
    transform_tables = (
        tables(num_tok, num_tok // 2, num_tok),
        tables(num_tok, inner_len, 2 * seq_total),
        tables(inner_len, inner_len, inner_len),
    )
    spread = (
        lax.all_to_all(carried, "ctx", split_axis=0, concat_axis=1, tiled=True),
        lax.all_to_all(filter_tok, "ctx", split_axis=0, concat_axis=1, tiled=True),
    )
    carried_chan = spread[0]
    filter_chan = spread[1]
    long_chan, spectra = convolve_forward(carried_chan, filter_chan, own_skip, transform_tables)
    long_tok = lax.all_to_all(long_chan, "ctx", split_axis=1, concat_axis=0, tiled=True)
    grad_chan = lax.all_to_all(grad_long, "ctx", split_axis=0, concat_axis=1, tiled=True)
    carried_grad_chan, filter_grad_chan = convolve_backward(
        grad_chan, spectra, own_skip, transform_tables
    )
    returned = (
        lax.all_to_all(carried_grad_chan, "ctx", split_axis=1, concat_axis=0, tiled=True),
        lax.all_to_all(filter_grad_chan, "ctx", split_axis=1, concat_axis=0, tiled=True),
    )
    carried_grad = returned[0]
    filter_grad_tok = returned[1]
    long_wide = long_tok.astype(jnp.float32)
    mixed = (query_feat * long_wide).astype(jnp.bfloat16)
    grad_query_feat = (grad_wide * long_wide).astype(jnp.bfloat16)
    grad_raw = filter_grad_tok.astype(jnp.float32) * envelope
    part_proj = jnp.dot(
        grad_raw, activation.T, precision=PRECISE, preferred_element_type=jnp.float32
    )
    grad_hidden = jnp.dot(
        filter_proj.T, grad_raw, precision=PRECISE, preferred_element_type=jnp.float32
    ) * jnp.cos(hidden_in)
    part_basis = jnp.dot(
        grad_hidden, basis_rows.T, precision=PRECISE, preferred_element_type=jnp.float32
    )
    grad_proj = lax.psum(part_proj, "ctx") * proj_scale
    grad_basis = lax.psum(part_basis, ("ctx", "tp")) * basis_scale
    carried_grad_wide = carried_grad.astype(jnp.float32)
    grad_key_feat = (carried_grad_wide * value_feat).astype(jnp.bfloat16)
    grad_value_feat = (carried_grad_wide * key_feat).astype(jnp.bfloat16)
    following = passed_along(
        (grad_query_feat[:, :rim_len], grad_key_feat[:, :rim_len], grad_value_feat[:, :rim_len]),
        "ctx",
        -1,
    )
    grad_query = featurize_back(grad_query_feat, following[0], short_kernel[0]).astype(jnp.bfloat16)
    grad_key = featurize_back(grad_key_feat, following[1], short_kernel[1]).astype(jnp.bfloat16)
    grad_value = featurize_back(grad_value_feat, following[2], short_kernel[2]).astype(jnp.bfloat16)
    return (mixed, grad_query, grad_key, grad_value, grad_proj, grad_basis)


def solution(mesh):
    return jax.shard_map(
        on_device,
        mesh=mesh,
        in_specs=(
            P("tp", "ctx"),
            P("tp", "ctx"),
            P("tp", "ctx"),
            P(None, "tp", None),
            P(),
            P(),
            P("tp", None),
            P("tp"),
            P("tp"),
            P("tp", "ctx"),
        ),
        out_specs=(
            P("tp", "ctx"),
            P("tp", "ctx"),
            P("tp", "ctx"),
            P("tp", "ctx"),
            P("tp", None),
            P(),
        ),
        check_vma=False,
    )
```

profile of v0, /device:TPU:1, one launch (start us, length us, event | category | flops | bytes accessed | tf_op | source)
XLA Modules:
  0.0 538.5 jit_solution(8369667688324918726)
XLA Ops:
  1.5 4.6 collective-permute-start
  10.4 15.5 %all-to-all-start = ((bf16[64,2,256]{2,1,0:T(2,128)(2,1)}), bf16[64,2,256]{2,1,0:T(2,128)(2,1)S(1)}, u32[]{:S(2)}, u32[]{:S(2)}) async-start(bf16[64,2,256]{2,1,0:T(2,128)(2,1)} %all_to_all.60), calls=%async_computation | async-start | bytes 131072 | tf_op jit(solution)/shard_map/all_to_all | solution.py:199
  26.0 3.5 collective-permute-start.2
  29.6 2.2 collective-permute-start.1
  35.7 2.4 all-to-all-done
  38.1 9.7 %all-to-all-start.3 = ((bf16[64,2,256]{2,1,0:T(2,128)(2,1)}), bf16[64,2,256]{2,1,0:T(2,128)(2,1)S(1)}, u32[]{:S(2)}, u32[]{:S(2)}) async-start(bf16[64,2,256]{2,1,0:T(2,128)(2,1)} %all_to_all.67), calls=%async_computation.3 | async-start | bytes 131072 | tf_op jit(solution)/shard_map/all_to_all | solution.py:205
  51.7 7.9 %all-to-all-done.3 = bf16[64,2,256]{2,1,0:T(2,128)(2,1)S(1)} async-done(((bf16[64,2,256]{2,1,0:T(2,128)(2,1)}), bf16[64,2,256]{2,1,0:T(2,128)(2,1)S(1)}, u32[]{:S(2)}, u32[]{:S(2)}) %all-to-all-start.3) | async-done | bytes 65568 | tf_op jit(solution)/shard_map/all_to_all | solution.py:205
  67.6 11.5 %fusion.19 = f32[2,128,128]{2,1,0:T(8,128)S(1)} fusion(f32[2,256,128]{1,2,0:T(8,128)S(1)} %convolution_subtract_fusion.1, f32[2,256,128]{1,2,0:T(8,128)S(1)} %convolution_add_fusion.1, f32[256,128]{0,1:T(8,128)S(1)} %copy.206, f32[256,128]{0,1:T(8,128)S(1)} %copy.204), kind=kOutput, calls=%fused_computation.45 | convolution fusion | flops 101318656 | bytes 917504 | tf_op jit(solution)/shard_map/kt,nks->nts/dot_general | solution.py:95
  80.9 4.8 all-to-all-start.4
  86.0 12.0 %all-to-all-done.4 = bf16[2,64,256]{2,0,1:T(2,128)(2,1)S(1)} async-done(((bf16[2,64,256]{2,0,1:T(2,128)(2,1)}), bf16[2,64,256]{2,0,1:T(2,128)(2,1)S(1)}, u32[]{:S(2)}, u32[]{:S(2)}) %all-to-all-start.4) | async-done | bytes 65568 | tf_op jit(solution)/shard_map/all_to_all | solution.py:210
  98.5 2.3 collective-permute-start.5
  101.9 6.0 %all-to-all-start.1 = ((bf16[64,2,256]{2,1,0:T(2,128)(2,1)}), bf16[64,2,256]{2,1,0:T(2,128)(2,1)S(1)}, u32[]{:S(2)}, u32[]{:S(2)}) async-start(bf16[64,2,256]{2,1,0:T(2,128)(2,1)} %all_to_all.63), calls=%async_computation.1 | async-start | bytes 131072 | tf_op jit(solution)/shard_map/all_to_all | solution.py:198
  108.0 2.4 collective-permute-start.4
  110.4 1.0 fusion.37
  111.4 2.1 collective-permute-done.4
  113.5 1.0 fusion.44
  114.5 5.6 %all-to-all-done.1 = bf16[64,2,256]{2,1,0:T(2,128)(2,1)S(1)} async-done(((bf16[64,2,256]{2,1,0:T(2,128)(2,1)}), bf16[64,2,256]{2,1,0:T(2,128)(2,1)S(1)}, u32[]{:S(2)}, u32[]{:S(2)}) %all-to-all-start.1) | async-done | bytes 65568 | tf_op jit(solution)/shard_map/all_to_all | solution.py:198
  130.0 7.0 %all-to-all-start.5 = ((bf16[2,64,256]{2,0,1:T(2,128)(2,1)}), bf16[2,64,256]{2,0,1:T(2,128)(2,1)S(1)}, u32[]{:S(2)}, u32[]{:S(2)}) async-start(bf16[2,64,256]{2,0,1:T(2,128)(2,1)} %copy.242), calls=%async_computation.5 | async-start | bytes 131072 | tf_op jit(solution)/shard_map/all_to_all | solution.py:211
  142.3 6.9 %all-to-all-done.5 = bf16[2,64,256]{2,0,1:T(2,128)(2,1)S(1)} async-done(((bf16[2,64,256]{2,0,1:T(2,128)(2,1)}), bf16[2,64,256]{2,0,1:T(2,128)(2,1)S(1)}, u32[]{:S(2)}, u32[]{:S(2)}) %all-to-all-start.5) | async-done | bytes 65568 | tf_op jit(solution)/shard_map/all_to_all | solution.py:211
  149.2 5.8 %all-to-all-start.2 = ((bf16[2,64,256]{2,0,1:T(2,128)(2,1)}), bf16[2,64,256]{2,0,1:T(2,128)(2,1)S(1)}, u32[]{:S(2)}, u32[]{:S(2)}) async-start(bf16[2,64,256]{2,0,1:T(2,128)(2,1)} %copy.223), calls=%async_computation.2 | async-start | bytes 131072 | tf_op jit(solution)/shard_map/all_to_all | solution.py:204
  156.2 99.6 %psum.15 = f32[64,33]{0,1:T(8,128)S(1)} all-reduce(f32[64,33]{0,1:T(8,128)S(1)} %fusion.423), channel_id=1, replica_groups=mesh['ctx'=64,'tp'=8] {'ctx','tp'}, use_global_device_ids=true, to_apply=%region_1.2 | all-reduce | flops 2112 | bytes 16896 | tf_op jit(solution)/shard_map/psum | solution.py:229
  255.8 270.7 %psum.14 = f32[128,64]{0,1:T(8,128)S(1)} all-reduce(f32[128,64]{0,1:T(8,128)S(1)} %fusion.417), channel_id=1, replica_groups=mesh['ctx'=64,'tp'=8] {'ctx'}, use_global_device_ids=true, to_apply=%region_0.1 | all-reduce | flops 8192 | bytes 65536 | tf_op jit(solution)/shard_map/psum | solution.py:228
  528.0 8.4 %collective-permute-start.3 = (bf16[128,6]{1,0:T(8,128)(2,1)S(1)}, bf16[128,6]{1,0:T(8,128)(2,1)S(1)}, u32[]{:S(2)}, u32[]{:S(2)}) collective-permute-start(bf16[128,6]{1,0:T(8,128)(2,1)S(1)} %slice.333), channel_id=1, source_target_pairs={{8,0},{16,8},{24,16},{32,24},{40,32},{48,40},{56,48},{64,56},{72,6... | collective-permute-start | bytes 4616 | tf_op jit(solution)/shard_map/ppermute | solution.py:13
  537.3 1.0 fusion.51
  (140 shorter events, 42.9 us)
Async XLA Ops:
  0.6 8.8 %copy-start = (f32[128,64]{0,1:T(8,128)S(1)}, f32[128,64]{0,1:T(8,128)}, u32[]{:S(2)}) copy-start(f32[128,64]{0,1:T(8,128)} %param.16) | copy-start | bytes 98308
  1.5 32.3 %collective-permute-start = (bf16[128,6]{1,0:T(8,128)(2,1)S(1)}, bf16[128,6]{1,0:T(8,128)(2,1)S(1)}, u32[]{:S(2)}, u32[]{:S(2)}) collective-permute-start(bf16[128,6]{1,0:T(8,128)(2,1)S(1)} %slice.242), channel_id=1, source_target_pairs={{0,8},{8,16},{16,24},{24,32},{32,40},{40,48},{48,56},{56,64},{64,7... | collective-permute-start | bytes 4616 | tf_op jit(solution)/shard_map/ppermute | solution.py:13
  7.5 0.7 copy-start.9
  8.2 0.7 copy-start.5
  8.2 0.7 copy-start.7
  10.4 15.5 %copy-start.3 = (bf16[128,256]{1,0:T(8,128)(2,1)S(1)}, bf16[128,256]{1,0:T(8,128)(2,1)}, u32[]{:S(2)}) copy-start(bf16[128,256]{1,0:T(8,128)(2,1)} %param.12) | copy-start | bytes 196612
  10.4 27.7 %all-to-all-start = ((bf16[64,2,256]{2,1,0:T(2,128)(2,1)}), bf16[64,2,256]{2,1,0:T(2,128)(2,1)S(1)}, u32[]{:S(2)}, u32[]{:S(2)}) async-start(bf16[64,2,256]{2,1,0:T(2,128)(2,1)} %all_to_all.60), calls=%async_computation | async-start | bytes 131072 | tf_op jit(solution)/shard_map/all_to_all | solution.py:199
  25.9 3.6 copy-start.4
  26.0 59.8 %collective-permute-start.2 = (bf16[128,6]{1,0:T(8,128)(2,1)S(1)}, bf16[128,6]{1,0:T(8,128)(2,1)S(1)}, u32[]{:S(2)}, u32[]{:S(2)}) collective-permute-start(bf16[128,6]{1,0:T(8,128)(2,1)S(1)} %slice.274), channel_id=1, source_target_pairs={{0,8},{8,16},{16,24},{24,32},{32,40},{40,48},{48,56},{56,64},{64,7... | collective-permute-start | bytes 4616 | tf_op jit(solution)/shard_map/ppermute | solution.py:13
  29.6 2.7 copy-start.6
  29.6 56.3 %collective-permute-start.1 = (bf16[128,6]{1,0:T(8,128)(2,1)S(1)}, bf16[128,6]{1,0:T(8,128)(2,1)S(1)}, u32[]{:S(2)}, u32[]{:S(2)}) collective-permute-start(bf16[128,6]{1,0:T(8,128)(2,1)S(1)} %slice.258), channel_id=1, source_target_pairs={{0,8},{8,16},{16,24},{24,32},{32,40},{40,48},{48,56},{56,64},{64,7... | collective-permute-start | bytes 4616 | tf_op jit(solution)/shard_map/ppermute | solution.py:13
  33.0 0.9 copy-start.2
  33.1 0.7 copy-start.8
  33.8 0.8 copy-start.1
  38.1 21.5 %all-to-all-start.3 = ((bf16[64,2,256]{2,1,0:T(2,128)(2,1)}), bf16[64,2,256]{2,1,0:T(2,128)(2,1)S(1)}, u32[]{:S(2)}, u32[]{:S(2)}) async-start(bf16[64,2,256]{2,1,0:T(2,128)(2,1)} %all_to_all.67), calls=%async_computation.3 | async-start | bytes 131072 | tf_op jit(solution)/shard_map/all_to_all | solution.py:205
  80.9 17.0 %all-to-all-start.4 = ((bf16[2,64,256]{2,0,1:T(2,128)(2,1)}), bf16[2,64,256]{2,0,1:T(2,128)(2,1)S(1)}, u32[]{:S(2)}, u32[]{:S(2)}) async-start(bf16[2,64,256]{2,0,1:T(2,128)(2,1)} %copy.236), calls=%async_computation.4 | async-start | bytes 131072 | tf_op jit(solution)/shard_map/all_to_all | solution.py:210
  98.5 11.8 %collective-permute-start.5 = (bf16[128,6]{1,0:T(8,128)(2,1)S(1)}, bf16[128,6]{1,0:T(8,128)(2,1)S(1)}, u32[]{:S(2)}, u32[]{:S(2)}) collective-permute-start(bf16[128,6]{1,0:T(8,128)(2,1)S(1)} %slice.349), channel_id=1, source_target_pairs={{8,0},{16,8},{24,16},{32,24},{40,32},{48,40},{56,48},{64,56},{72,6... | collective-permute-start | bytes 4616 | tf_op jit(solution)/shard_map/ppermute | solution.py:13
  101.9 18.2 %all-to-all-start.1 = ((bf16[64,2,256]{2,1,0:T(2,128)(2,1)}), bf16[64,2,256]{2,1,0:T(2,128)(2,1)S(1)}, u32[]{:S(2)}, u32[]{:S(2)}) async-start(bf16[64,2,256]{2,1,0:T(2,128)(2,1)} %all_to_all.63), calls=%async_computation.1 | async-start | bytes 131072 | tf_op jit(solution)/shard_map/all_to_all | solution.py:198
  108.0 5.5 %collective-permute-start.4 = (bf16[128,6]{1,0:T(8,128)(2,1)S(1)}, bf16[128,6]{1,0:T(8,128)(2,1)S(1)}, u32[]{:S(2)}, u32[]{:S(2)}) collective-permute-start(bf16[128,6]{1,0:T(8,128)(2,1)S(1)} %slice.341), channel_id=1, source_target_pairs={{8,0},{16,8},{24,16},{32,24},{40,32},{48,40},{56,48},{64,56},{72,6... | collective-permute-start | bytes 4616 | tf_op jit(solution)/shard_map/ppermute | solution.py:13
  130.0 19.1 %all-to-all-start.5 = ((bf16[2,64,256]{2,0,1:T(2,128)(2,1)}), bf16[2,64,256]{2,0,1:T(2,128)(2,1)S(1)}, u32[]{:S(2)}, u32[]{:S(2)}) async-start(bf16[2,64,256]{2,0,1:T(2,128)(2,1)} %copy.242), calls=%async_computation.5 | async-start | bytes 131072 | tf_op jit(solution)/shard_map/all_to_all | solution.py:211
  149.2 378.0 %all-to-all-start.2 = ((bf16[2,64,256]{2,0,1:T(2,128)(2,1)}), bf16[2,64,256]{2,0,1:T(2,128)(2,1)S(1)}, u32[]{:S(2)}, u32[]{:S(2)}) async-start(bf16[2,64,256]{2,0,1:T(2,128)(2,1)} %copy.223), calls=%async_computation.2 | async-start | bytes 131072 | tf_op jit(solution)/shard_map/all_to_all | solution.py:204
  528.0 9.3 %collective-permute-start.3 = (bf16[128,6]{1,0:T(8,128)(2,1)S(1)}, bf16[128,6]{1,0:T(8,128)(2,1)S(1)}, u32[]{:S(2)}, u32[]{:S(2)}) collective-permute-start(bf16[128,6]{1,0:T(8,128)(2,1)S(1)} %slice.333), channel_id=1, source_target_pairs={{8,0},{16,8},{24,16},{32,24},{40,32},{48,40},{56,48},{64,56},{72,6... | collective-permute-start | bytes 4616 | tf_op jit(solution)/shard_map/ppermute | solution.py:13
where the time goes:
time: 544 us; the launch traced here: 539 us
  blocking collectives  370 us (68%)
  starting transfers between devices  72.2 us (13%)
  matrix products  39.1 us (7%)
  waiting for transfers between devices  37.1 us (7%)
  other arithmetic  9.16 us (2%)
  local copies, waits for them, and re-layouts  8.96 us (2%)
    psum x1, blocking collectives, on_device(): grad_proj = lax.psum(part_proj, 'ctx') * proj_scale  271 us
    psum x1, blocking collectives, on_device(): grad_basis = lax.psum(part_basis, ('ctx', 'tp')) * basis_scale  99.6 us
    ppermute x6, starting transfers between devices, passed_along(): lax.ppermute(value, axis, [(source, source + steps) for source in range(l...  23.4 us
    all_to_all x1, starting transfers between devices, on_device(): lax.all_to_all(filter_tok, 'ctx', split_axis=0, concat_axis=1, tiled=True)  15.5 us
    dot_general x3, matrix products, restore(): jnp.einsum('kt,nks->nts', outer[0], turned_re, precision=PRECISE)  13.3 us
    all_to_all x1, waiting for transfers between devices, on_device(): lax.all_to_all(carried_grad_chan, 'ctx', split_axis=1, concat_axis=0, til...  12 us
  transfers between devices with their start and end apart: 12, of which 7 were waited for; matrix products, arithmetic and copies ran while one was open for 7% of the time, Pallas kernels for 0%

commit v1 on v0

--- a/solution.py
+++ b/solution.py
@@ -5,6 +5,12 @@
 from jax.sharding import PartitionSpec as P
 
 PRECISE = lax.Precision.HIGHEST
+
+
+def trade_parts(x, name, split, join):
+    parts = jnp.split(x, lax.axis_size(name), axis=split)
+    arrived = lax.all_to_all(jnp.stack(parts), name, 0, 0)
+    return jnp.concatenate(arrived, axis=join)
 
 
 def passed_along(value, axis, steps):
@@ -208,7 +214,7 @@
     )
     returned = (
         lax.all_to_all(carried_grad_chan, "ctx", split_axis=1, concat_axis=0, tiled=True),
-        lax.all_to_all(filter_grad_chan, "ctx", split_axis=1, concat_axis=0, tiled=True),
+        trade_parts(filter_grad_chan, "ctx", 1, 0),
     )
     carried_grad = returned[0]
     filter_grad_tok = returned[1]

time: 544 us -> 580 us (1.066)
  local copies, waits for them, and re-layouts: 8.96 us -> 44.4 us
    unnamed x20 -> x84, local copies, waits for them, and re-layouts: 2.66 us -> 38.3 us
where the time goes in v1:
time: 580 us; the launch traced here: 574 us
  blocking collectives  370 us (64%)
  starting transfers between devices  72.2 us (12%)
  local copies, waits for them, and re-layouts  44.4 us (8%)
  matrix products  39.4 us (7%)
  waiting for transfers between devices  37.1 us (6%)
  other arithmetic  9.12 us (2%)
    psum x1, blocking collectives, on_device(): grad_proj = lax.psum(part_proj, 'ctx') * proj_scale  271 us
    psum x1, blocking collectives, on_device(): grad_basis = lax.psum(part_basis, ('ctx', 'tp')) * basis_scale  99.6 us
    unnamed x84, local copies, waits for them, and re-layouts  38.3 us
    ppermute x6, starting transfers between devices, passed_along(): lax.ppermute(value, axis, [(source, source + steps) for source in range(l...  23.4 us
    all_to_all x1, starting transfers between devices, on_device(): lax.all_to_all(filter_tok, 'ctx', split_axis=0, concat_axis=1, tiled=True)  15.5 us
    dot_general x3, matrix products, restore(): jnp.einsum('kt,nks->nts', outer[0], turned_re, precision=PRECISE)  13.6 us
    all_to_all x1, waiting for transfers between devices, on_device(): lax.all_to_all(carried_grad_chan, 'ctx', split_axis=1, concat_axis=0, til...  12 us
  transfers between devices with their start and end apart: 12, of which 7 were waited for; matrix products, arithmetic and copies ran while one was open for 7% of the time, Pallas kernels for 0%

profile of v1, /device:TPU:1, one launch (start us, length us, event | category | flops | bytes accessed | tf_op | source)
XLA Modules:
  0.0 574.3 jit_solution(5328795821849559709)
XLA Ops:
  1.5 4.6 collective-permute-start
  10.4 15.5 %all-to-all-start = ((bf16[64,2,256]{2,1,0:T(2,128)(2,1)}), bf16[64,2,256]{2,1,0:T(2,128)(2,1)S(1)}, u32[]{:S(2)}, u32[]{:S(2)}) async-start(bf16[64,2,256]{2,1,0:T(2,128)(2,1)} %all_to_all.55), calls=%async_computation | async-start | bytes 131072 | tf_op jit(solution)/shard_map/all_to_all | solution.py:205
  26.0 3.5 collective-permute-start.2
  29.6 2.2 collective-permute-start.1
  35.7 2.4 all-to-all-done
  38.1 9.7 %all-to-all-start.3 = ((bf16[64,2,256]{2,1,0:T(2,128)(2,1)}), bf16[64,2,256]{2,1,0:T(2,128)(2,1)S(1)}, u32[]{:S(2)}, u32[]{:S(2)}) async-start(bf16[64,2,256]{2,1,0:T(2,128)(2,1)} %all_to_all.62), calls=%async_computation.3 | async-start | bytes 131072 | tf_op jit(solution)/shard_map/all_to_all | solution.py:211
  51.7 7.9 %all-to-all-done.3 = bf16[64,2,256]{2,1,0:T(2,128)(2,1)S(1)} async-done(((bf16[64,2,256]{2,1,0:T(2,128)(2,1)}), bf16[64,2,256]{2,1,0:T(2,128)(2,1)S(1)}, u32[]{:S(2)}, u32[]{:S(2)}) %all-to-all-start.3) | async-done | bytes 65568 | tf_op jit(solution)/shard_map/all_to_all | solution.py:211
  67.6 11.9 %fusion.19 = f32[2,128,128]{2,1,0:T(8,128)S(1)} fusion(f32[2,256,128]{1,2,0:T(8,128)S(1)} %convolution_subtract_fusion.1, f32[2,256,128]{1,2,0:T(8,128)S(1)} %convolution_add_fusion.1, f32[256,128]{0,1:T(8,128)S(1)} %copy.202, f32[256,128]{0,1:T(8,128)S(1)} %copy.200), kind=kOutput, calls=%fused_computation.45 | convolution fusion | flops 101318656 | bytes 917504 | tf_op jit(solution)/shard_map/kt,nks->nts/dot_general | solution.py:101
  81.3 4.8 all-to-all-start.4
  86.4 12.0 %all-to-all-done.4 = bf16[2,64,256]{2,0,1:T(2,128)(2,1)S(1)} async-done(((bf16[2,64,256]{2,0,1:T(2,128)(2,1)}), bf16[2,64,256]{2,0,1:T(2,128)(2,1)S(1)}, u32[]{:S(2)}, u32[]{:S(2)}) %all-to-all-start.4) | async-done | bytes 65568 | tf_op jit(solution)/shard_map/all_to_all | solution.py:216
  98.9 2.3 collective-permute-start.5
  102.3 6.0 %all-to-all-start.1 = ((bf16[64,2,256]{2,1,0:T(2,128)(2,1)}), bf16[64,2,256]{2,1,0:T(2,128)(2,1)S(1)}, u32[]{:S(2)}, u32[]{:S(2)}) async-start(bf16[64,2,256]{2,1,0:T(2,128)(2,1)} %all_to_all.58), calls=%async_computation.1 | async-start | bytes 131072 | tf_op jit(solution)/shard_map/all_to_all | solution.py:204
  108.3 2.4 collective-permute-start.4
  110.7 1.0 fusion.37
  111.8 2.1 collective-permute-done.4
  113.9 1.0 fusion.44
  114.9 5.6 all-to-all-done.1
  165.9 7.0 %all-to-all-start.5 = ((bf16[64,2,256]{2,1,0:T(2,128)(2,1)}), bf16[64,2,256]{2,1,0:T(2,128)(2,1)S(1)}, u32[]{:S(2)}, u32[]{:S(2)}) async-start(bf16[64,2,256]{2,1,0:T(2,128)(2,1)} %constant_dynamic-update-slice_fusion), calls=%async_computation.5 | async-start | bytes 131072 | tf_op jit(solution)/shard_map/all_to_all | solution.py:12
  178.1 6.9 %all-to-all-done.5 = bf16[64,2,256]{2,1,0:T(2,128)(2,1)S(1)} async-done(((bf16[64,2,256]{2,1,0:T(2,128)(2,1)}), bf16[64,2,256]{2,1,0:T(2,128)(2,1)S(1)}, u32[]{:S(2)}, u32[]{:S(2)}) %all-to-all-start.5) | async-done | bytes 65568 | tf_op jit(solution)/shard_map/all_to_all | solution.py:12
  185.1 5.8 %all-to-all-start.2 = ((bf16[2,64,256]{2,0,1:T(2,128)(2,1)}), bf16[2,64,256]{2,0,1:T(2,128)(2,1)S(1)}, u32[]{:S(2)}, u32[]{:S(2)}) async-start(bf16[2,64,256]{2,0,1:T(2,128)(2,1)} %copy.219), calls=%async_computation.2 | async-start | bytes 131072 | tf_op jit(solution)/shard_map/all_to_all | solution.py:210
  191.9 99.6 %psum.15 = f32[64,33]{0,1:T(8,128)S(1)} all-reduce(f32[64,33]{0,1:T(8,128)S(1)} %fusion.423), channel_id=1, replica_groups=mesh['ctx'=64,'tp'=8] {'ctx','tp'}, use_global_device_ids=true, to_apply=%region_1.2 | all-reduce | flops 2112 | bytes 16896 | tf_op jit(solution)/shard_map/psum | solution.py:235
  291.6 270.7 %psum.14 = f32[128,64]{0,1:T(8,128)S(1)} all-reduce(f32[128,64]{0,1:T(8,128)S(1)} %fusion.417), channel_id=1, replica_groups=mesh['ctx'=64,'tp'=8] {'ctx'}, use_global_device_ids=true, to_apply=%region_0.1 | all-reduce | flops 8192 | bytes 65536 | tf_op jit(solution)/shard_map/psum | solution.py:234
  563.7 8.4 %collective-permute-start.3 = (bf16[128,6]{1,0:T(8,128)(2,1)S(1)}, bf16[128,6]{1,0:T(8,128)(2,1)S(1)}, u32[]{:S(2)}, u32[]{:S(2)}) collective-permute-start(bf16[128,6]{1,0:T(8,128)(2,1)S(1)} %slice.333), channel_id=1, source_target_pairs={{8,0},{16,8},{24,16},{32,24},{40,32},{48,40},{56,48},{64,56},{72,6... | collective-permute-start | bytes 4616 | tf_op jit(solution)/shard_map/ppermute | solution.py:19
  573.0 1.0 fusion.51
  (202 shorter events, 78.2 us)
Async XLA Ops:
  0.6 8.8 %copy-start = (f32[128,64]{0,1:T(8,128)S(1)}, f32[128,64]{0,1:T(8,128)}, u32[]{:S(2)}) copy-start(f32[128,64]{0,1:T(8,128)} %param.16) | copy-start | bytes 98308
  1.5 32.3 %collective-permute-start = (bf16[128,6]{1,0:T(8,128)(2,1)S(1)}, bf16[128,6]{1,0:T(8,128)(2,1)S(1)}, u32[]{:S(2)}, u32[]{:S(2)}) collective-permute-start(bf16[128,6]{1,0:T(8,128)(2,1)S(1)} %slice.242), channel_id=1, source_target_pairs={{0,8},{8,16},{16,24},{24,32},{32,40},{40,48},{48,56},{56,64},{64,7... | collective-permute-start | bytes 4616 | tf_op jit(solution)/shard_map/ppermute | solution.py:19
  7.5 0.7 copy-start.9
  8.2 0.7 copy-start.5
  8.2 0.7 copy-start.7
  10.4 15.5 %copy-start.3 = (bf16[128,256]{1,0:T(8,128)(2,1)S(1)}, bf16[128,256]{1,0:T(8,128)(2,1)}, u32[]{:S(2)}) copy-start(bf16[128,256]{1,0:T(8,128)(2,1)} %param.12) | copy-start | bytes 196612
  10.4 27.7 %all-to-all-start = ((bf16[64,2,256]{2,1,0:T(2,128)(2,1)}), bf16[64,2,256]{2,1,0:T(2,128)(2,1)S(1)}, u32[]{:S(2)}, u32[]{:S(2)}) async-start(bf16[64,2,256]{2,1,0:T(2,128)(2,1)} %all_to_all.55), calls=%async_computation | async-start | bytes 131072 | tf_op jit(solution)/shard_map/all_to_all | solution.py:205
  25.9 3.6 copy-start.4
  26.0 60.2 %collective-permute-start.2 = (bf16[128,6]{1,0:T(8,128)(2,1)S(1)}, bf16[128,6]{1,0:T(8,128)(2,1)S(1)}, u32[]{:S(2)}, u32[]{:S(2)}) collective-permute-start(bf16[128,6]{1,0:T(8,128)(2,1)S(1)} %slice.274), channel_id=1, source_target_pairs={{0,8},{8,16},{16,24},{24,32},{32,40},{40,48},{48,56},{56,64},{64,7... | collective-permute-start | bytes 4616 | tf_op jit(solution)/shard_map/ppermute | solution.py:19
  29.6 2.7 copy-start.6
  29.6 56.6 %collective-permute-start.1 = (bf16[128,6]{1,0:T(8,128)(2,1)S(1)}, bf16[128,6]{1,0:T(8,128)(2,1)S(1)}, u32[]{:S(2)}, u32[]{:S(2)}) collective-permute-start(bf16[128,6]{1,0:T(8,128)(2,1)S(1)} %slice.258), channel_id=1, source_target_pairs={{0,8},{8,16},{16,24},{24,32},{32,40},{40,48},{48,56},{56,64},{64,7... | collective-permute-start | bytes 4616 | tf_op jit(solution)/shard_map/ppermute | solution.py:19
  33.0 0.9 copy-start.2
  33.1 0.7 copy-start.8
  33.8 0.8 copy-start.1
  38.1 21.5 %all-to-all-start.3 = ((bf16[64,2,256]{2,1,0:T(2,128)(2,1)}), bf16[64,2,256]{2,1,0:T(2,128)(2,1)S(1)}, u32[]{:S(2)}, u32[]{:S(2)}) async-start(bf16[64,2,256]{2,1,0:T(2,128)(2,1)} %all_to_all.62), calls=%async_computation.3 | async-start | bytes 131072 | tf_op jit(solution)/shard_map/all_to_all | solution.py:211
  81.3 17.0 %all-to-all-start.4 = ((bf16[2,64,256]{2,0,1:T(2,128)(2,1)}), bf16[2,64,256]{2,0,1:T(2,128)(2,1)S(1)}, u32[]{:S(2)}, u32[]{:S(2)}) async-start(bf16[2,64,256]{2,0,1:T(2,128)(2,1)} %copy.232), calls=%async_computation.4 | async-start | bytes 131072 | tf_op jit(solution)/shard_map/all_to_all | solution.py:216
  98.9 11.8 %collective-permute-start.5 = (bf16[128,6]{1,0:T(8,128)(2,1)S(1)}, bf16[128,6]{1,0:T(8,128)(2,1)S(1)}, u32[]{:S(2)}, u32[]{:S(2)}) collective-permute-start(bf16[128,6]{1,0:T(8,128)(2,1)S(1)} %slice.349), channel_id=1, source_target_pairs={{8,0},{16,8},{24,16},{32,24},{40,32},{48,40},{56,48},{64,56},{72,6... | collective-permute-start | bytes 4616 | tf_op jit(solution)/shard_map/ppermute | solution.py:19
  102.3 18.2 %all-to-all-start.1 = ((bf16[64,2,256]{2,1,0:T(2,128)(2,1)}), bf16[64,2,256]{2,1,0:T(2,128)(2,1)S(1)}, u32[]{:S(2)}, u32[]{:S(2)}) async-start(bf16[64,2,256]{2,1,0:T(2,128)(2,1)} %all_to_all.58), calls=%async_computation.1 | async-start | bytes 131072 | tf_op jit(solution)/shard_map/all_to_all | solution.py:204
  108.3 5.5 collective-permute-start.4
  165.9 19.1 %all-to-all-start.5 = ((bf16[64,2,256]{2,1,0:T(2,128)(2,1)}), bf16[64,2,256]{2,1,0:T(2,128)(2,1)S(1)}, u32[]{:S(2)}, u32[]{:S(2)}) async-start(bf16[64,2,256]{2,1,0:T(2,128)(2,1)} %constant_dynamic-update-slice_fusion), calls=%async_computation.5 | async-start | bytes 131072 | tf_op jit(solution)/shard_map/all_to_all | solution.py:12
  185.1 377.8 %all-to-all-start.2 = ((bf16[2,64,256]{2,0,1:T(2,128)(2,1)}), bf16[2,64,256]{2,0,1:T(2,128)(2,1)S(1)}, u32[]{:S(2)}, u32[]{:S(2)}) async-start(bf16[2,64,256]{2,0,1:T(2,128)(2,1)} %copy.219), calls=%async_computation.2 | async-start | bytes 131072 | tf_op jit(solution)/shard_map/all_to_all | solution.py:210
  563.7 9.3 %collective-permute-start.3 = (bf16[128,6]{1,0:T(8,128)(2,1)S(1)}, bf16[128,6]{1,0:T(8,128)(2,1)S(1)}, u32[]{:S(2)}, u32[]{:S(2)}) collective-permute-start(bf16[128,6]{1,0:T(8,128)(2,1)S(1)} %slice.333), channel_id=1, source_target_pairs={{8,0},{16,8},{24,16},{32,24},{40,32},{48,40},{56,48},{64,56},{72,6... | collective-permute-start | bytes 4616 | tf_op jit(solution)/shard_map/ppermute | solution.py:19
